TPU v7x, 256 devices: a whole 4x4x8 slice. The times are simulated.
256 devices in a mesh: dp: 8 (over x, y_lo), tensor: 32 (over z, y_hi, core).
Axes of the slice: x: 4, y: 4 (y_hi: 2, y_lo: 2; y = y_hi * 2 + y_lo), z: 8, core: 2. Of those that a mesh axis runs over, the one named last changes fastest.
Arguments:
- real_feats: bfloat16 [16384, 1536], P(('dp', 'tensor')), may hold values from -6 to 6
- fake_feats: bfloat16 [16384, 1536], P(('dp', 'tensor')), may hold values from -6 to 6
- mix_num: int32 [16384], P(('dp', 'tensor')), may hold values from 0 to 256
- w_first: bfloat16 [1536, 12288], P(None, 'tensor'), may hold values from -0.15625 to 0.15625
- bias: float32 [12288], P('tensor'), may hold values from -3 to 3
- head: float32 [12288], P('tensor'), may hold values from -0.0546875 to 0.0546875
Outputs:
- grad_w: float32 [1536, 12288], P('dp', 'tensor')
- grad_bias: float32 [12288], P('tensor')
- grad_head: float32 [12288], P('tensor')
- penalty: float32 [], replicated
All inputs are finite; a program needn't handle non-finite values.
Results may differ from a plain program's by a relative error of at most 0.0005.
Values may be sent and summed in bfloat16 or wider, within the bound.
No kernel may reach another device: no remote copies, remote signals or barrier semaphores. Data moves between devices by JAX's collectives and lax.ppermute only.
A program may use at most 64 MiB of HBM per device.

v0:
```python
import jax
import jax.numpy as jnp
from jax import lax
from jax.sharding import Mesh
from jax.sharding import PartitionSpec as P

TENSOR = ("tensor_0", "tensor_1", "tensor_2")
DP_TENSOR = ("dp", "tensor_0", "tensor_1", "tensor_2")


def sent_to_all(array, axis):
    copies = jnp.broadcast_to(array, (lax.axis_size(axis), *array.shape))
    return lax.all_to_all(copies, axis, split_axis=0, concat_axis=0, tiled=True)


def over_copies(array, axis):
    everything = sent_to_all(array, axis)
    return jnp.sum(everything, axis=0)


def in_order(tiles, dim):
    lengths = list(tiles.shape[1:])
    lengths[dim] *= tiles.shape[0]
    return jnp.moveaxis(tiles, 0, dim).reshape(lengths)


def gather_in_order(array, axes, order):
    tiles = array
    for k in order:
        tiles = lax.all_gather(tiles, axes[k])
    done = order[::-1]
    back = [done.index(k) for k in range(len(axes))]
    tiles = tiles.transpose(*back, *range(len(axes), tiles.ndim))
    return tiles.reshape(-1, *array.shape)


def whole_of(array, axes, order, dim):
    return in_order(gather_in_order(array, axes, order), dim)


def cut_along(array, dim, length):
    lengths = array.shape
    tiles = array.reshape(*lengths[:dim], length, lengths[dim] // length, *lengths[dim + 1 :])
    return jnp.moveaxis(tiles, dim, 0)


def sum_at_owner(array, axis, dim):
    length = lax.axis_size(axis)
    tiles = lax.all_to_all(cut_along(array, dim, length), axis, 0, 0, tiled=True)
    return jnp.sum(tiles, axis=0)


def packed_total(arrays, axis):
    ravelled, at, finished = (jnp.concatenate([a.reshape(-1) for a in arrays]), 0, [])
    running = over_copies(ravelled, axis)
    for a in arrays:
        finished.append(running[at : at + a.size].reshape(a.shape))
        at += a.size
    return tuple(finished)


def row_contract(left, right):
    return lax.dot_general(
        left, right, (((0,), (0,)), ((), ())), preferred_element_type=jnp.float32
    )


def local(real_feats, fake_feats, mix_num, w_first, bias, head):
    coef = mix_num.astype(jnp.float32) / 256.0
    real_f = real_feats.astype(jnp.float32)
    mixed = (real_f + coef[:, None] * (fake_feats.astype(jnp.float32) - real_f)).astype(
        jnp.bfloat16
    )
    group = lax.all_gather(mixed, TENSOR, axis=0, tiled=True)
    z = jnp.dot(group, w_first, preferred_element_type=jnp.float32) + bias
    sg = jax.nn.sigmoid(z)
    d1 = sg * (1.0 + z * (1.0 - sg))
    d2 = sg * (1.0 - sg) * (2.0 + z * (1.0 - 2.0 * sg))
    u = (d1 * head).astype(jnp.bfloat16)
    total_rows = group.shape[0] * lax.axis_size("dp")
    whole = lax.dot_general(
        u, w_first, (((1,), (1,)), ((), ())), preferred_element_type=jnp.float32
    )
    grad_cols = lax.psum_scatter(
        whole.astype(jnp.bfloat16), TENSOR, scatter_dimension=1, tiled=True
    ).astype(jnp.float32)
    squares = over_copies(jnp.sum(grad_cols * grad_cols, axis=1), TENSOR)
    norm = jnp.sqrt(squares + 1e-06)
    scale = 20.0 * (norm - 1.0) / norm
    scaled_cols = (scale[:, None] * grad_cols).astype(jnp.bfloat16)
    loss = over_copies(jnp.sum((norm - 1.0) ** 2), "dp")
    big = whole_of(scaled_cols, TENSOR, (1, 0, 2), 1)
    penalty = 10.0 * loss / total_rows
    p = jnp.dot(big, w_first, preferred_element_type=jnp.float32)
    dz = p * head * d2
    dzb = dz.astype(jnp.bfloat16)
    partial_w = row_contract(group, dzb)
    partial_w = partial_w + row_contract(big, u)
    grad_w = sum_at_owner(partial_w, "dp", 0)
    grad_bias, grad_head = packed_total((jnp.sum(dz, axis=0), jnp.sum(p * d1, axis=0)), "dp")
    return (grad_w, grad_bias, grad_head, penalty)


def solution(mesh):
    torus = Mesh(
        mesh.devices.reshape(mesh.shape["dp"], 8, 2, 2), ("dp", "tensor_0", "tensor_1", "tensor_2")
    )
    return jax.shard_map(
        local,
        mesh=torus,
        in_specs=(
            P(DP_TENSOR, None),
            P(DP_TENSOR, None),
            P(DP_TENSOR),
            P(None, TENSOR),
            P(TENSOR),
            P(TENSOR),
        ),
        out_specs=(P("dp", TENSOR), P(TENSOR), P(TENSOR), P()),
        check_vma=False,
    )
```

profile of v0, /device:TPU:1, one launch (start us, length us, event | category | flops | bytes accessed | tf_op | source)
XLA Modules:
  0.0 429.0 jit_solution(8761464536619151029)
XLA Ops:
  7.2 0.0 copy-start
  7.2 0.0 all-gather.7.cloned.1.call-start
  7.2 0.7 convert_multiply_fusion.2
  8.0 1.8 fusion.7
  9.8 0.0 all-gather.7.cloned.1.call-update
  9.8 0.0 copy-start.3
  9.8 0.0 copy-start.4
  9.8 0.0 reduce-scatter.2.cloned.1.call-start
  9.9 99.4 %all-gather.7.cloned.1.call-done = bf16[2048,1536]{1,0:T(8,128)(2,1)} async-done(((bf16[64,1536]{1,0:T(8,128)(2,1)}), bf16[2048,1536]{1,0:T(8,128)(2,1)}) %all-gather.7.cloned.1.call-update) | async-done | bytes 6291472 | tf_op jit(solution)/shard_map/all_gather | solution.py:74
  109.3 0.0 copy-done
  109.3 5.5 %fusion.15 = f32[2048,384]{1,0:T(8,128)S(1)} fusion(bf16[2048,1536]{1,0:T(8,128)(2,1)} %all-gather.7.cloned.1.call-done, bf16[1536,384]{1,0:T(8,128)(2,1)S(1)} %copy-done), kind=kOutput, calls=%fused_computation.29 | convolution fusion | flops 2415919104 | bytes 10616832 | tf_op jit(solution)/shard_map/dot_general | solution.py:75
  114.7 0.0 copy-start.5
  114.7 1.6 copy-done.5
  116.4 0.0 copy-done.3
  116.4 0.0 copy-done.4
  116.4 5.7 %convolution_convert_fusion = bf16[2048,1536]{0,1:T(8,128)(2,1)} fusion(bf16[1536,384]{1,0:T(8,128)(2,1)S(1)} %copy-done, f32[384]{0:T(512)S(1)} %copy-done.4, f32[2048,384]{1,0:T(8,128)S(1)} %fusion.15, f32[384]{0:T(512)S(1)} %copy-done.3), kind=kOutput, calls=%fused_computation | convolution fusion | flops 2426929152 | bytes 10619904 | tf_op jit(solution)/shard_map/dot_general | solution.py:81
  122.1 0.0 reduce-scatter.2.cloned.1.call-update
  122.1 0.0 all-gather.9.cloned.1.call-start
  122.1 129.7 %reduce-scatter.2.cloned.1.call-done = bf16[2048,48]{0,1:T(8,128)(2,1)} async-done(((bf16[2048,1536]{0,1:T(8,128)(2,1)}), bf16[2048,48]{0,1:T(8,128)(2,1)}) %reduce-scatter.2.cloned.1.call-update) | async-done | bytes 196624 | tf_op jit(solution)/shard_map/reduce_scatter | solution.py:84
  251.9 1.0 fusion.8
  252.9 0.1 broadcast_in_dim.6
  253.0 23.0 %all_to_all.23 = f32[32,1,2048]{2,1,0:T(1,128)S(1)} all-to-all(f32[32,1,2048]{2,1,0:T(1,128)S(1)} %broadcast_in_dim.6), channel_id=1, replica_groups=mesh['dp'=8,'tensor_0'=8,'tensor_1'=2,'tensor_2'=2] {'tensor_0','tensor_..., dimensions={0} | all-to-all | bytes 524288 | tf_op jit(solution)/shard_map/all_to_all | solution.py:13
  276.0 0.2 reduce_sum.73
  276.2 0.6 multiply_reduce_fusion.1
  276.8 1.0 fusion.9
  277.8 8.2 %all-gather = bf16[4096,48]{0,1:T(8,128)(2,1)S(1)} all-gather(bf16[2048,48]{0,1:T(8,128)(2,1)S(1)} %fusion.9), channel_id=2, replica_groups=mesh['dp'=8,'tensor_0'=8,'tensor_1'=2,'tensor_2'=2] {'tensor_1'}, dimensions={0}, use_global_device_ids=true | all-gather | bytes 589824 | tf_op jit(solution)/shard_map/all_gather | solution.py:30
  286.0 0.8 copy.28
  286.8 0.0 all-gather.9.cloned.1.call-update
  286.8 0.0 all-gather.11.cloned.1.call-start
  286.8 41.3 %all-gather.9.cloned.1.call-done = bf16[16,2048,48]{1,2,0:T(8,128)(2,1)} async-done(((bf16[2,2048,48]{1,2,0:T(8,128)(2,1)}), bf16[16,2048,48]{1,2,0:T(8,128)(2,1)}) %all-gather.9.cloned.1.call-update) | async-done | bytes 3145744 | tf_op jit(solution)/shard_map/all_gather | solution.py:30
  328.1 0.0 all-gather.11.cloned.1.call-update
  328.1 1.2 broadcast_in_dim.16
  329.4 4.9 %all-to-all-start.3 = ((f32[8,1,1]{2,1,0:T(1,128)}), f32[8,1,1]{2,1,0:T(1,128)S(1)}, u32[]{:S(2)}, u32[]{:S(2)}) async-start(f32[8,1,1]{2,1,0:T(1,128)} %broadcast_in_dim.16), calls=%async_computation.4 | async-start | bytes 8192 | tf_op jit(solution)/shard_map/all_to_all | solution.py:13
  334.3 17.5 %all-gather.11.cloned.1.call-done = bf16[16,2,2048,48]{2,3,1,0:T(8,128)(2,1)} async-done(((bf16[8,2,2048,48]{2,3,1,0:T(8,128)(2,1)}), bf16[16,2,2048,48]{2,3,1,0:T(8,128)(2,1)}) %all-gather.11.cloned.1.call-update) | async-done | bytes 6291472 | tf_op jit(solution)/shard_map/all_gather | solution.py:30
  351.8 0.0 copy-start.6
  351.8 0.0 slice-start
  351.8 3.5 copy.18
  355.3 0.0 copy-start.1
  355.3 0.1 copy-done.6
  355.5 0.0 slice-start.1
  355.5 5.4 %fusion.12 = (f32[384]{0:T(512)S(1)}, bf16[2048,384]{1,0:T(8,128)(2,1)S(1)}, f32[384]{0:T(512)S(1)}) fusion(f32[2048,384]{1,0:T(8,128)S(1)} %copy-done.6, f32[384]{0:T(512)S(1)} %copy-done.3, f32[384]{0:T(512)S(1)} %copy-done.4, bf16[2048,1536]{0,1:T(8,128)(2,1)S(1)} %bitcast.22, bf16[1536,384]{1,0:T(8,128)(2,1)S(1)} %copy-done), kind=kOutput, calls=%fused_computation.27 | convolution fusion | flops 2431646720 | bytes 12195840 | tf_op jit(solution)/shard_map/dot_general | solution.py:94
  360.9 0.0 copy-done.1
  360.9 0.0 slice-done
  360.9 0.0 slice-done.1
  361.0 4.9 %fusion.4 = f32[1536,384]{1,0:T(8,128)} fusion(bf16[2048,1536]{1,0:T(8,128)(2,1)S(1)} %bitcast.30, bf16[2048,384]{1,0:T(8,128)(2,1)S(1)} %get-tuple-element.5), kind=kOutput, calls=%fused_computation.11 | convolution fusion | flops 2415919104 | bytes 10223616 | tf_op jit(solution)/shard_map/dot_general | solution.py:63
  365.8 0.0 all-to-all-done.3
  365.8 0.6 broadcast_in_dim.7
  366.5 4.6 %all-to-all-start.2 = ((f32[8,1,768]{2,1,0:T(1,128)}), f32[8,1,768]{2,1,0:T(1,128)S(1)}, u32[]{:S(2)}, u32[]{:S(2)}) async-start(f32[8,1,768]{2,1,0:T(1,128)} %broadcast_in_dim.7), calls=%async_computation.3 | async-start | bytes 49152 | tf_op jit(solution)/shard_map/all_to_all | solution.py:13
  371.1 9.4 %convolution_add_fusion = f32[1536,384]{1,0:T(8,128)} fusion(f32[1536,384]{1,0:T(8,128)} %fusion.4, bf16[2048,1536]{0,1:T(8,128)(2,1)} %bitcast.23, f32[384]{0:T(512)S(1)} %copy-done.4, f32[2048,384]{1,0:T(8,128)} %copy-done.5, f32[384]{0:T(512)S(1)} %copy-done.3), kind=kOutput, calls=%fused_computation.10 | convolution fusion | flops 2424373248 | bytes 14158848 | tf_op jit(solution)/shard_map/dot_general | solution.py:63
  380.5 0.0 all-to-all-done.2
  380.5 0.0 copy-start.2
  380.5 0.6 copy-done.2
  381.1 5.1 %all-to-all-start.1 = ((f32[8,192,384]{2,1,0:T(8,128)}), f32[8,192,384]{2,1,0:T(8,128)S(1)}, u32[]{:S(2)}, u32[]{:S(2)}) async-start(f32[8,192,384]{2,1,0:T(8,128)} %bitcast.26), calls=%async_computation.2 | async-start | bytes 4718592 | tf_op jit(solution)/shard_map/all_to_all | solution.py:49
  386.3 0.6 reduce_sum.79
  387.5 0.8 reduce_sum.77
  388.3 0.6 fusion.14
  388.9 31.6 %all-to-all-done.1 = f32[8,192,384]{2,1,0:T(8,128)S(1)} async-done(((f32[8,192,384]{2,1,0:T(8,128)}), f32[8,192,384]{2,1,0:T(8,128)S(1)}, u32[]{:S(2)}, u32[]{:S(2)}) %all-to-all-start.1) | async-done | bytes 2359328 | tf_op jit(solution)/shard_map/all_to_all | solution.py:49
  420.5 0.8 reduce_sum.74
  (2 shorter events, 0.0 us)
Async XLA Ops:
  7.2 102.1 %copy-start = (bf16[1536,384]{1,0:T(8,128)(2,1)S(1)}, bf16[1536,384]{1,0:T(8,128)(2,1)}, u32[]{:S(2)}) copy-start(bf16[1536,384]{1,0:T(8,128)(2,1)} %param.9) | copy-start | bytes 3538948
  7.2 102.1 %all-gather.7.cloned.1.call-start = ((), (), s32[]{:S(2)}) async-start(), calls=%async_computation.5 | async-start | bytes 6488064 | tf_op jit(solution)/shard_map/all_gather | solution.py:74
  9.8 106.6 %copy-start.3 = (f32[384]{0:T(512)S(1)}, f32[384]{0:T(512)}, u32[]{:S(2)}) copy-start(f32[384]{0:T(512)} %param.10) | copy-start | bytes 4612
  9.8 106.6 %copy-start.4 = (f32[384]{0:T(512)S(1)}, f32[384]{0:T(512)}, u32[]{:S(2)}) copy-start(f32[384]{0:T(512)} %param.11) | copy-start | bytes 4612
  9.8 242.0 %reduce-scatter.2.cloned.1.call-start = ((), (), s32[]{:S(2)}) async-start(), calls=%async_computation.6 | async-start | bytes 6488064 | tf_op jit(solution)/shard_map/reduce_scatter | solution.py:84
  114.7 1.6 copy-start.5
  122.1 206.0 %all-gather.9.cloned.1.call-start = ((), (), s32[]{:S(2)}) async-start(), calls=%async_computation.7 | async-start | bytes 3538944 | tf_op jit(solution)/shard_map/all_gather | solution.py:30
  286.8 65.0 %all-gather.11.cloned.1.call-start = ((), (), s32[]{:S(2)}) async-start(), calls=%async_computation.8 | async-start | bytes 9437184 | tf_op jit(solution)/shard_map/all_gather | solution.py:30
  329.4 36.5 %all-to-all-start.3 = ((f32[8,1,1]{2,1,0:T(1,128)}), f32[8,1,1]{2,1,0:T(1,128)S(1)}, u32[]{:S(2)}, u32[]{:S(2)}) async-start(f32[8,1,1]{2,1,0:T(1,128)} %broadcast_in_dim.16), calls=%async_computation.4 | async-start | bytes 8192 | tf_op jit(solution)/shard_map/all_to_all | solution.py:13
  351.8 3.7 copy-start.6
  351.8 9.2 %slice-start = ((s8[6291456]{0:T(1024)(128)(4,1)}), s8[4194304]{0:T(1024)(128)(4,1)S(1)}, s32[]{:S(2)}) async-start(s8[6291456]{0:T(1024)(128)(4,1)} %bitcast.29), calls=%async_computation.9 | async-start | bytes 8388608
  355.3 5.6 %copy-start.1 = (bf16[8,2,2,2048,48]{3,4,2,1,0:T(8,128)(2,1)}, bf16[8,2,2,2048,48]{3,4,2,1,0:T(8,128)(2,1)S(1)}, u32[]{:S(2)}) copy-start(bf16[8,2,2,2048,48]{3,4,2,1,0:T(8,128)(2,1)S(1)} %copy.18) | copy-start | bytes 18874372
  355.5 5.5 %slice-start.1 = ((s8[6291456]{0:T(1024)(128)(4,1)}), s8[2097152]{0:T(1024)(128)(4,1)S(1)}, s32[]{:S(2)}) async-start(s8[6291456]{0:T(1024)(128)(4,1)} %bitcast.29), calls=%async_computation.10 | async-start | bytes 4194304
  366.5 14.0 %all-to-all-start.2 = ((f32[8,1,768]{2,1,0:T(1,128)}), f32[8,1,768]{2,1,0:T(1,128)S(1)}, u32[]{:S(2)}, u32[]{:S(2)}) async-start(f32[8,1,768]{2,1,0:T(1,128)} %broadcast_in_dim.7), calls=%async_computation.3 | async-start | bytes 49152 | tf_op jit(solution)/shard_map/all_to_all | solution.py:13
  380.5 0.6 copy-start.2
  381.1 39.4 %all-to-all-start.1 = ((f32[8,192,384]{2,1,0:T(8,128)}), f32[8,192,384]{2,1,0:T(8,128)S(1)}, u32[]{:S(2)}, u32[]{:S(2)}) async-start(f32[8,192,384]{2,1,0:T(8,128)} %bitcast.26), calls=%async_computation.2 | async-start | bytes 4718592 | tf_op jit(solution)/shard_map/all_to_all | solution.py:49
Sparse Core Ops, SparseCore 0:
  11.3 97.8 all-gather.6
  122.2 129.6 reduce-scatter.1
  286.9 41.1 all-gather.8
  329.7 21.9 all-gather.10
where the time goes:
time: 429 us
  waiting for transfers between devices  320 us (75%)
  blocking collectives  31.2 us (7%)
  matrix products  30.9 us (7%)
  between operations  15.7 us (4%)
  starting transfers between devices  14.8 us (3%)
  local copies, waits for them, and re-layouts  9.31 us (2%)
  other arithmetic  7.51 us (2%)
    reduce_scatter x1, waiting for transfers between devices, local(): lax.psum_scatter(whole.astype(jnp.bfloat16), TENSOR, scatter_dimension=1,...  130 us
    all_gather x1, waiting for transfers between devices, local(): group = lax.all_gather(mixed, TENSOR, axis=0, tiled=True)  99.4 us
    all_gather x2, waiting for transfers between devices, gather_in_order(): tiles = lax.all_gather(tiles, axes[k])  58.8 us
    all_to_all x1, waiting for transfers between devices, sum_at_owner(): lax.all_to_all(cut_along(array, dim, length), axis, 0, 0, tiled=True)  31.6 us
    all_to_all x1, blocking collectives, sent_to_all(): return lax.all_to_all(copies, axis, split_axis=0, concat_axis=0, tiled=True)  23 us
    dot_general x2, matrix products, row_contract(): lax.dot_general(left, right, (((0,), (0,)), ((), ())), preferred_element_...  14.3 us
    all_to_all x2, starting transfers between devices, sent_to_all(): return lax.all_to_all(copies, axis, split_axis=0, concat_axis=0, tiled=True)  9.52 us
  transfers between devices with their start and end apart: 7, of which 5 were waited for; matrix products, arithmetic and copies ran while one was open for 6% of the time, Pallas kernels for 0%

commit v1 on v0

--- a/solution.py
+++ b/solution.py
@@ -71,7 +71,9 @@
     mixed = (real_f + coef[:, None] * (fake_feats.astype(jnp.float32) - real_f)).astype(
         jnp.bfloat16
     )
-    group = lax.all_gather(mixed, TENSOR, axis=0, tiled=True)
+    group = jnp.concatenate(
+        lax.all_to_all(jnp.stack([mixed] * lax.axis_size(TENSOR)), TENSOR, 0, 0), axis=0
+    )
     z = jnp.dot(group, w_first, preferred_element_type=jnp.float32) + bias
     sg = jax.nn.sigmoid(z)
     d1 = sg * (1.0 + z * (1.0 - sg))

time: 429 us -> 484 us (1.13)
  blocking collectives: 31.2 us -> 184 us
  waiting for transfers between devices: 320 us -> 221 us
    all_to_all x0 -> x1, blocking collectives: none -> 153 us  [local(): lax.all_to_all(jnp.stack([mixed] * lax.axis_size(TENSOR)), TENSOR, 0, 0)]
    all_gather x1 -> x0, waiting for transfers between devices: 99.4 us -> none  [local(): group = lax.all_gather(mixed, TENSOR, axis=0, tiled=True)]
  transfers between devices with their start and end apart: 7 -> 6, of which waited for: 5 -> 4; matrix products, arithmetic and copies ran while one was open for 6% -> 5% of each run, Pallas kernels for 0% -> 0%
where the time goes in v1:
time: 484 us
  waiting for transfers between devices  221 us (46%)
  blocking collectives  184 us (38%)
  matrix products  28.8 us (6%)
  between operations  15.6 us (3%)
  starting transfers between devices  14.8 us (3%)
  local copies, waits for them, and re-layouts  12.7 us (3%)
  other arithmetic  6.83 us (1%)
    all_to_all x1, blocking collectives, local(): lax.all_to_all(jnp.stack([mixed] * lax.axis_size(TENSOR)), TENSOR, 0, 0)  153 us
    reduce_scatter x1, waiting for transfers between devices, local(): lax.psum_scatter(whole.astype(jnp.bfloat16), TENSOR, scatter_dimension=1,...  130 us
    all_gather x2, waiting for transfers between devices, gather_in_order(): tiles = lax.all_gather(tiles, axes[k])  58.9 us
    all_to_all x1, waiting for transfers between devices, sum_at_owner(): lax.all_to_all(cut_along(array, dim, length), axis, 0, 0, tiled=True)  31.6 us
    all_to_all x1, blocking collectives, sent_to_all(): return lax.all_to_all(copies, axis, split_axis=0, concat_axis=0, tiled=True)  23 us
    dot_general x2, matrix products, row_contract(): lax.dot_general(left, right, (((0,), (0,)), ((), ())), preferred_element_...  14.3 us
  transfers between devices with their start and end apart: 6, of which 4 were waited for; matrix products, arithmetic and copies ran while one was open for 5% of the time, Pallas kernels for 0%

profile of v1, /device:TPU:1, one launch (start us, length us, event | category | flops | bytes accessed | tf_op | source)
XLA Modules:
  0.0 483.9 jit_solution(15541710794639571504)
XLA Ops:
  7.2 0.0 copy-start
  7.2 0.0 reduce-scatter.2.cloned.1.call-start
  7.2 0.7 convert_multiply_fusion.2
  8.0 1.1 fusion.7
  9.1 0.7 stack.2
  9.8 153.0 %all_to_all.28 = bf16[32,64,1536]{2,1,0:T(8,128)(2,1)S(1)} all-to-all(bf16[32,64,1536]{2,1,0:T(8,128)(2,1)S(1)} %stack.2), channel_id=1, replica_groups=mesh['dp'=8,'tensor_0'=8,'tensor_1'=2,'tensor_2'=2] {'tensor_0','tensor_..., dimensions={0} | all-to-all | bytes 12582912 | tf_op jit(solution)/shard_map/all_to_all | solution.py:75
  162.8 0.0 copy-start.1
  162.8 2.6 copy-done.1
  165.4 0.0 copy-done
  165.4 0.0 copy-start.4
  165.4 0.0 copy-start.5
  165.4 3.4 fusion.15
  168.9 0.0 copy-start.6
  168.9 1.6 copy-done.6
  170.5 0.0 copy-done.4
  170.5 0.0 copy-done.5
  170.5 5.7 %convolution_convert_fusion = bf16[2048,1536]{0,1:T(8,128)(2,1)} fusion(bf16[1536,384]{1,0:T(8,128)(2,1)S(1)} %copy-done, f32[384]{0:T(512)S(1)} %copy-done.5, f32[2048,384]{1,0:T(8,128)S(1)} %fusion.15, f32[384]{0:T(512)S(1)} %copy-done.4), kind=kOutput, calls=%fused_computation | convolution fusion | flops 2426929152 | bytes 10619904 | tf_op jit(solution)/shard_map/dot_general | solution.py:83
  176.2 0.0 reduce-scatter.2.cloned.1.call-update
  176.2 0.0 all-gather.6.cloned.1.call-start
  176.3 130.4 %reduce-scatter.2.cloned.1.call-done = bf16[2048,48]{0,1:T(8,128)(2,1)} async-done(((bf16[2048,1536]{0,1:T(8,128)(2,1)}), bf16[2048,48]{0,1:T(8,128)(2,1)}) %reduce-scatter.2.cloned.1.call-update) | async-done | bytes 196624 | tf_op jit(solution)/shard_map/reduce_scatter | solution.py:86
  306.7 1.0 fusion.8
  307.6 0.1 broadcast_in_dim.6
  307.8 23.0 %all_to_all.29 = f32[32,1,2048]{2,1,0:T(1,128)S(1)} all-to-all(f32[32,1,2048]{2,1,0:T(1,128)S(1)} %broadcast_in_dim.6), channel_id=1, replica_groups=mesh['dp'=8,'tensor_0'=8,'tensor_1'=2,'tensor_2'=2] {'tensor_0','tensor_..., dimensions={0} | all-to-all | bytes 524288 | tf_op jit(solution)/shard_map/all_to_all | solution.py:13
  330.8 0.2 reduce_sum.73
  331.0 0.6 multiply_reduce_fusion.1
  331.6 1.0 fusion.9
  332.5 8.2 %all-gather = bf16[4096,48]{0,1:T(8,128)(2,1)S(1)} all-gather(bf16[2048,48]{0,1:T(8,128)(2,1)S(1)} %fusion.9), channel_id=2, replica_groups=mesh['dp'=8,'tensor_0'=8,'tensor_1'=2,'tensor_2'=2] {'tensor_1'}, dimensions={0}, use_global_device_ids=true | all-gather | bytes 589824 | tf_op jit(solution)/shard_map/all_gather | solution.py:30
  340.8 0.8 copy.28
  341.5 0.0 all-gather.6.cloned.1.call-update
  341.6 0.0 all-gather.8.cloned.1.call-start
  341.6 41.2 %all-gather.6.cloned.1.call-done = bf16[16,2048,48]{1,2,0:T(8,128)(2,1)} async-done(((bf16[2,2048,48]{1,2,0:T(8,128)(2,1)}), bf16[16,2048,48]{1,2,0:T(8,128)(2,1)}) %all-gather.6.cloned.1.call-update) | async-done | bytes 3145744 | tf_op jit(solution)/shard_map/all_gather | solution.py:30
  382.8 0.0 all-gather.8.cloned.1.call-update
  382.9 1.2 broadcast_in_dim.16
  384.1 4.9 %all-to-all-start.4 = ((f32[8,1,1]{2,1,0:T(1,128)}), f32[8,1,1]{2,1,0:T(1,128)S(1)}, u32[]{:S(2)}, u32[]{:S(2)}) async-start(f32[8,1,1]{2,1,0:T(1,128)} %broadcast_in_dim.16), calls=%async_computation.5 | async-start | bytes 8192 | tf_op jit(solution)/shard_map/all_to_all | solution.py:13
  389.0 17.7 %all-gather.8.cloned.1.call-done = bf16[16,2,2048,48]{2,3,1,0:T(8,128)(2,1)} async-done(((bf16[8,2,2048,48]{2,3,1,0:T(8,128)(2,1)}), bf16[16,2,2048,48]{2,3,1,0:T(8,128)(2,1)}) %all-gather.8.cloned.1.call-update) | async-done | bytes 6291472 | tf_op jit(solution)/shard_map/all_gather | solution.py:30
  406.7 0.0 copy-start.7
  406.7 0.0 slice-start
  406.7 3.5 copy.18
  410.2 0.0 copy-start.2
  410.2 0.1 copy-done.7
  410.4 0.0 slice-start.1
  410.4 5.4 %fusion.12 = (f32[384]{0:T(512)S(1)}, bf16[2048,384]{1,0:T(8,128)(2,1)S(1)}, f32[384]{0:T(512)S(1)}) fusion(f32[2048,384]{1,0:T(8,128)S(1)} %copy-done.7, f32[384]{0:T(512)S(1)} %copy-done.4, f32[384]{0:T(512)S(1)} %copy-done.5, bf16[2048,1536]{0,1:T(8,128)(2,1)S(1)} %bitcast.27, bf16[1536,384]{1,0:T(8,128)(2,1)S(1)} %copy-done), kind=kOutput, calls=%fused_computation.27 | convolution fusion | flops 2431646720 | bytes 12195840 | tf_op jit(solution)/shard_map/dot_general | solution.py:96
  415.8 0.0 copy-done.2
  415.8 0.0 slice-done
  415.8 0.0 slice-done.1
  415.8 4.9 %fusion.4 = f32[1536,384]{1,0:T(8,128)} fusion(bf16[2048,1536]{1,0:T(8,128)(2,1)S(1)} %bitcast.26, bf16[2048,384]{1,0:T(8,128)(2,1)S(1)} %get-tuple-element.5), kind=kOutput, calls=%fused_computation.11 | convolution fusion | flops 2415919104 | bytes 10223616 | tf_op jit(solution)/shard_map/dot_general | solution.py:63
  420.7 0.0 all-to-all-done.4
  420.8 0.6 broadcast_in_dim.7
  421.4 4.6 all-to-all-start.3
  426.0 9.4 %convolution_add_fusion = f32[1536,384]{1,0:T(8,128)} fusion(f32[1536,384]{1,0:T(8,128)} %fusion.4, bf16[2048,1536]{0,1:T(8,128)(2,1)} %bitcast.28, f32[384]{0:T(512)S(1)} %copy-done.5, f32[2048,384]{1,0:T(8,128)} %copy-done.6, f32[384]{0:T(512)S(1)} %copy-done.4), kind=kOutput, calls=%fused_computation.10 | convolution fusion | flops 2424373248 | bytes 14158848 | tf_op jit(solution)/shard_map/dot_general | solution.py:63
  435.4 0.0 all-to-all-done.3
  435.4 0.0 copy-start.3
  435.4 0.6 copy-done.3
  436.0 5.2 %all-to-all-start.2 = ((f32[8,192,384]{2,1,0:T(8,128)}), f32[8,192,384]{2,1,0:T(8,128)S(1)}, u32[]{:S(2)}, u32[]{:S(2)}) async-start(f32[8,192,384]{2,1,0:T(8,128)} %bitcast.31), calls=%async_computation.3 | async-start | bytes 4718592 | tf_op jit(solution)/shard_map/all_to_all | solution.py:49
  441.2 0.6 reduce_sum.79
  442.4 0.8 reduce_sum.77
  443.2 0.6 fusion.14
  443.8 31.6 %all-to-all-done.2 = f32[8,192,384]{2,1,0:T(8,128)S(1)} async-done(((f32[8,192,384]{2,1,0:T(8,128)}), f32[8,192,384]{2,1,0:T(8,128)S(1)}, u32[]{:S(2)}, u32[]{:S(2)}) %all-to-all-start.2) | async-done | bytes 2359328 | tf_op jit(solution)/shard_map/all_to_all | solution.py:49
  475.4 0.8 reduce_sum.74
  (2 shorter events, 0.0 us)
Async XLA Ops:
  7.2 158.3 %copy-start = (bf16[1536,384]{1,0:T(8,128)(2,1)S(1)}, bf16[1536,384]{1,0:T(8,128)(2,1)}, u32[]{:S(2)}) copy-start(bf16[1536,384]{1,0:T(8,128)(2,1)} %param.9) | copy-start | bytes 3538948
  7.2 299.5 %reduce-scatter.2.cloned.1.call-start = ((), (), s32[]{:S(2)}) async-start(), calls=%async_computation.6 | async-start | bytes 6488064 | tf_op jit(solution)/shard_map/reduce_scatter | solution.py:86
  162.8 2.6 copy-start.1
  165.4 5.1 %copy-start.4 = (f32[384]{0:T(512)S(1)}, f32[384]{0:T(512)}, u32[]{:S(2)}) copy-start(f32[384]{0:T(512)} %param.10) | copy-start | bytes 4612
  165.4 5.1 %copy-start.5 = (f32[384]{0:T(512)S(1)}, f32[384]{0:T(512)}, u32[]{:S(2)}) copy-start(f32[384]{0:T(512)} %param.11) | copy-start | bytes 4612
  168.9 1.6 copy-start.6
  176.2 206.6 %all-gather.6.cloned.1.call-start = ((), (), s32[]{:S(2)}) async-start(), calls=%async_computation.7 | async-start | bytes 3538944 | tf_op jit(solution)/shard_map/all_gather | solution.py:30
  341.6 65.1 %all-gather.8.cloned.1.call-start = ((), (), s32[]{:S(2)}) async-start(), calls=%async_computation.8 | async-start | bytes 9437184 | tf_op jit(solution)/shard_map/all_gather | solution.py:30
  384.1 36.6 %all-to-all-start.4 = ((f32[8,1,1]{2,1,0:T(1,128)}), f32[8,1,1]{2,1,0:T(1,128)S(1)}, u32[]{:S(2)}, u32[]{:S(2)}) async-start(f32[8,1,1]{2,1,0:T(1,128)} %broadcast_in_dim.16), calls=%async_computation.5 | async-start | bytes 8192 | tf_op jit(solution)/shard_map/all_to_all | solution.py:13
  406.7 3.7 copy-start.7
  406.7 9.1 %slice-start = ((s8[6291456]{0:T(1024)(128)(4,1)}), s8[2097152]{0:T(1024)(128)(4,1)S(1)}, s32[]{:S(2)}) async-start(s8[6291456]{0:T(1024)(128)(4,1)} %bitcast.24), calls=%async_computation.9 | async-start | bytes 4194304
  410.2 5.6 %copy-start.2 = (bf16[8,2,2,2048,48]{3,4,2,1,0:T(8,128)(2,1)}, bf16[8,2,2,2048,48]{3,4,2,1,0:T(8,128)(2,1)S(1)}, u32[]{:S(2)}) copy-start(bf16[8,2,2,2048,48]{3,4,2,1,0:T(8,128)(2,1)S(1)} %copy.18) | copy-start | bytes 18874372
  410.4 5.4 %slice-start.1 = ((s8[6291456]{0:T(1024)(128)(4,1)}), s8[4194304]{0:T(1024)(128)(4,1)S(1)}, s32[]{:S(2)}) async-start(s8[6291456]{0:T(1024)(128)(4,1)} %bitcast.24), calls=%async_computation.10 | async-start | bytes 8388608
  421.4 14.0 %all-to-all-start.3 = ((f32[8,1,768]{2,1,0:T(1,128)}), f32[8,1,768]{2,1,0:T(1,128)S(1)}, u32[]{:S(2)}, u32[]{:S(2)}) async-start(f32[8,1,768]{2,1,0:T(1,128)} %broadcast_in_dim.7), calls=%async_computation.4 | async-start | bytes 49152 | tf_op jit(solution)/shard_map/all_to_all | solution.py:13
  435.4 0.6 copy-start.3
  436.0 39.4 %all-to-all-start.2 = ((f32[8,192,384]{2,1,0:T(8,128)}), f32[8,192,384]{2,1,0:T(8,128)S(1)}, u32[]{:S(2)}, u32[]{:S(2)}) async-start(f32[8,192,384]{2,1,0:T(8,128)} %bitcast.31), calls=%async_computation.3 | async-start | bytes 4718592 | tf_op jit(solution)/shard_map/all_to_all | solution.py:49
Sparse Core Ops, SparseCore 0:
  176.3 130.2 reduce-scatter.1
  341.7 41.1 all-gather.5
  384.6 21.9 all-gather.7
